TPU v7x, 1024 devices: a whole 4x4x32 slice. The times are simulated.
1024 devices in a mesh: wide: 16 (over x, y_hi, core), narrow: 64 (over z, y_lo).
Axes of the slice: x: 4, y: 4 (y_hi: 2, y_lo: 2; y = y_hi * 2 + y_lo), z: 32, core: 2. Of those that a mesh axis runs over, the one named last changes fastest.
Arguments:
- state: float32 [2, 33554432], P(None, ('wide', 'narrow')), may hold values from -6 to 6
- gates: float32 [6, 2, 128, 128], replicated, may hold values from -0.375 to 0.375
Outputs:
- amplitudes: float32 [2, 33554432], P(None, ('wide', 'narrow'))
All inputs are finite; a program needn't handle non-finite values.
Results may differ from a plain program's by a relative error of at most 0.0001.
Values sent between devices are 32-bit elements; how exact they have to be, the bound alone decides.
A program may use at most 32 MiB of HBM per device.

v0:
```python
import jax
import jax.numpy as jnp
from jax import lax
from jax.sharding import PartitionSpec as P


def from_partner(value, axis, bit):
    mask = 2**bit
    pairs = [(source, source ^ mask) for source in range(lax.axis_size(axis))]
    return lax.ppermute(value, axis, pairs)


def apply_gate(amplitudes, joined_gate):
    gate_dim = joined_gate.shape[-1]
    columns = amplitudes.shape[1] // gate_dim
    shaped = amplitudes.reshape(2, gate_dim, columns)
    matrix = jnp.stack(
        [jnp.stack([joined_gate[0], -joined_gate[1]]), jnp.stack([joined_gate[1], joined_gate[0]])]
    )
    result = jnp.einsum("cir,kcji->krj", shaped, matrix, precision=lax.Precision.HIGHEST)
    return result.reshape(2, columns * gate_dim)


def remap_wide(amplitudes):
    wide_count = lax.axis_size("wide")
    current = amplitudes
    for bit_number in range(wide_count.bit_length() - 1):
        upper_count = wide_count >> bit_number + 1
        lower_count = 1 << bit_number
        shaped = current.reshape(2, upper_count, 2, lower_count, -1)
        own_bit = lax.axis_index("wide") >> bit_number & 1
        leaving = lax.dynamic_slice_in_dim(shaped, 1 - own_bit, 1, 2)
        arrived = from_partner(leaving, "wide", bit_number)
        marker = lax.broadcasted_iota(jnp.int32, (1, 1, 2, 1, 1), 2)
        current = jnp.where(marker == own_bit, shaped, arrived).reshape(amplitudes.shape)
    return current


def remap_narrow(amplitudes):
    wide_count = lax.axis_size("wide")
    narrow_count = lax.axis_size("narrow")
    shaped = amplitudes.reshape(2, wide_count, narrow_count, -1)
    moved = lax.all_to_all(shaped, "narrow", split_axis=2, concat_axis=2, tiled=True)
    return moved.reshape(amplitudes.shape)


def on_device(state, gates):
    amplitudes = state
    layers_total = gates.shape[0] // 2
    for layer_index in range(layers_total):
        amplitudes = apply_gate(amplitudes, gates[2 * layer_index])
        amplitudes = apply_gate(amplitudes, gates[2 * layer_index + 1])
        if layer_index + 1 < layers_total:
            amplitudes = remap_narrow(remap_wide(amplitudes))
    return amplitudes


def solution(mesh):
    return jax.shard_map(
        on_device,
        mesh=mesh,
        in_specs=(P(None, ("wide", "narrow")), P()),
        out_specs=P(None, ("wide", "narrow")),
        check_vma=False,
    )
```

profile of v0, /device:TPU:24, one launch (start us, length us, event | category | flops | bytes accessed | tf_op | source)
XLA Modules:
  0.0 204.2 jit_solution(1033295856490145928)
XLA Ops:
  0.0 2.0 slice_bitcast_fusion.10
  5.0 1.9 collective-permute-start
  7.1 1.1 collective-permute-done
  8.8 3.1 %collective-permute-start.1 = (f32[2,4,1,2,2048]{4,3,2,1,0:T(2,128)S(1)}, f32[2,4,1,2,2048]{4,3,2,1,0:T(2,128)S(1)}, u32[]{:S(2)}, u32[]{:S(2)}) collective-permute-start(f32[2,4,1,2,2048]{4,3,2,1,0:T(2,128)S(1)} %dynamic-slice_select_fusion.11), channel_id=1, source_target_pairs={{0,128},{64,192},{128,0},{192,64},{256,384},{320,448},{384,256},{4... | collective-permute-start | bytes 393224 | tf_op jit(solution)/shard_map/ppermute | solution.py:10
  12.7 5.1 %collective-permute-done.1 = f32[2,4,1,2,2048]{4,3,2,1,0:T(2,128)S(1)} collective-permute-done((f32[2,4,1,2,2048]{4,3,2,1,0:T(2,128)S(1)}, f32[2,4,1,2,2048]{4,3,2,1,0:T(2,128)S(1)}, u32[]{:S(2)}, u32[]{:S(2)}) %collective-permute-start.1) | collective-permute-done | bytes 131104 | tf_op jit(solution)/shard_map/ppermute | solution.py:10
  18.2 3.4 %collective-permute-start.2 = (f32[2,2,1,4,2048]{4,3,2,1,0:T(4,128)S(1)}, f32[2,2,1,4,2048]{4,3,2,1,0:T(4,128)S(1)}, u32[]{:S(2)}, u32[]{:S(2)}) collective-permute-start(f32[2,2,1,4,2048]{4,3,2,1,0:T(4,128)S(1)} %dynamic-slice_select_fusion.9), channel_id=1, source_target_pairs={{0,256},{64,320},{128,384},{192,448},{256,0},{320,64},{384,128},{4... | collective-permute-start | bytes 393224 | tf_op jit(solution)/shard_map/ppermute | solution.py:10
  22.5 2.7 %collective-permute-done.2 = f32[2,2,1,4,2048]{4,3,2,1,0:T(4,128)S(1)} collective-permute-done((f32[2,2,1,4,2048]{4,3,2,1,0:T(4,128)S(1)}, f32[2,2,1,4,2048]{4,3,2,1,0:T(4,128)S(1)}, u32[]{:S(2)}, u32[]{:S(2)}) %collective-permute-start.2) | collective-permute-done | bytes 131104 | tf_op jit(solution)/shard_map/ppermute | solution.py:10
  26.0 4.9 %collective-permute-start.3 = (f32[2,1,1,8,2048]{4,3,2,0,1:T(8,128)}, f32[2,1,1,8,2048]{4,3,2,0,1:T(8,128)}, u32[]{:S(2)}, u32[]{:S(2)}) collective-permute-start(f32[2,1,1,8,2048]{4,3,2,0,1:T(8,128)} %dynamic-slice_select_fusion.6), channel_id=1, source_target_pairs={{0,512},{64,576},{128,640},{192,704},{256,768},{320,832},{384,896}... | collective-permute-start | bytes 393224 | tf_op jit(solution)/shard_map/ppermute | solution.py:10
  34.3 1.4 broadcast_in_dim.224
  35.7 1.4 broadcast_in_dim.231
  38.1 1.3 broadcast_in_dim.240
  39.4 2.2 %select_select_fusion.1 = f32[2,16,64,32]{3,2,1,0:T(8,128)S(1)} fusion(f32[2,16,64,32]{3,2,1,0:T(8,128)} %broadcast_in_dim.240, f32[2,16,64,32]{3,2,1,0:T(8,128)} %broadcast_in_dim.231, f32[2,16,64,32]{3,2,1,0:T(8,128)} %broadcast_in_dim.224, f32[2,16,64,32]{3,2,1,0:T(8,128)S(1)} %reshape_reshape.46, f32[2,16,64,32]{3,2,1,0:T(8,128)S(1)} %broadcast_in_dim.220, ...), kind=kLoop, calls=%fused_computation.7 | loop fusion | flops 262144 | bytes 1572928 | tf_op jit(solution)/shard_map/jit(_where)/select_n | solution.py:35
  42.3 1.2 reshape.288
  43.4 30.5 %all-to-all-start = ((f32[64,1,1024]{2,1,0:T(1,128)}), f32[64,1,1024]{2,1,0:T(1,128)S(1)}, u32[]{:S(2)}, u32[]{:S(2)}) async-start(f32[64,1,1024]{2,1,0:T(1,128)} %reshape.288), calls=%async_computation | async-start | bytes 524288 | tf_op jit(solution)/shard_map/all_to_all | solution.py:43
  74.1 40.3 %all-to-all-done = f32[64,1,1024]{2,1,0:T(1,128)S(1)} async-done(((f32[64,1,1024]{2,1,0:T(1,128)}), f32[64,1,1024]{2,1,0:T(1,128)S(1)}, u32[]{:S(2)}, u32[]{:S(2)}) %all-to-all-start) | async-done | bytes 262176 | tf_op jit(solution)/shard_map/all_to_all | solution.py:43
  114.8 1.2 reduce.2
  118.6 2.1 %collective-permute-start.4 = (f32[2,8,1,1,2048]{4,2,1,0,3:T(1,128)S(1)}, f32[2,8,1,1,2048]{4,2,1,0,3:T(1,128)S(1)}, u32[]{:S(2)}, u32[]{:S(2)}) collective-permute-start(f32[2,8,1,1,2048]{4,2,1,0,3:T(1,128)S(1)} %constant_dynamic-slice_fusion.1), channel_id=1, source_target_pairs={{0,64},{64,0},{128,192},{192,128},{256,320},{320,256},{384,448},{4... | collective-permute-start | bytes 393224 | tf_op jit(solution)/shard_map/ppermute | solution.py:10
  120.9 1.0 collective-permute-done.4
  122.5 3.1 %collective-permute-start.5 = (f32[2,4,1,2,2048]{4,3,2,1,0:T(2,128)S(1)}, f32[2,4,1,2,2048]{4,3,2,1,0:T(2,128)S(1)}, u32[]{:S(2)}, u32[]{:S(2)}) collective-permute-start(f32[2,4,1,2,2048]{4,3,2,1,0:T(2,128)S(1)} %dynamic-slice_select_fusion.5), channel_id=1, source_target_pairs={{0,128},{64,192},{128,0},{192,64},{256,384},{320,448},{384,256},{4... | collective-permute-start | bytes 393224 | tf_op jit(solution)/shard_map/ppermute | solution.py:10
  126.1 5.3 %collective-permute-done.5 = f32[2,4,1,2,2048]{4,3,2,1,0:T(2,128)S(1)} collective-permute-done((f32[2,4,1,2,2048]{4,3,2,1,0:T(2,128)S(1)}, f32[2,4,1,2,2048]{4,3,2,1,0:T(2,128)S(1)}, u32[]{:S(2)}, u32[]{:S(2)}) %collective-permute-start.5) | collective-permute-done | bytes 131104 | tf_op jit(solution)/shard_map/ppermute | solution.py:10
  131.9 2.5 %collective-permute-start.6 = (f32[2,2,1,4,2048]{4,3,2,1,0:T(4,128)S(1)}, f32[2,2,1,4,2048]{4,3,2,1,0:T(4,128)S(1)}, u32[]{:S(2)}, u32[]{:S(2)}) collective-permute-start(f32[2,2,1,4,2048]{4,3,2,1,0:T(4,128)S(1)} %dynamic-slice_select_fusion.3), channel_id=1, source_target_pairs={{0,256},{64,320},{128,384},{192,448},{256,0},{320,64},{384,128},{4... | collective-permute-start | bytes 393224 | tf_op jit(solution)/shard_map/ppermute | solution.py:10
  134.8 3.9 %collective-permute-done.6 = f32[2,2,1,4,2048]{4,3,2,1,0:T(4,128)S(1)} collective-permute-done((f32[2,2,1,4,2048]{4,3,2,1,0:T(4,128)S(1)}, f32[2,2,1,4,2048]{4,3,2,1,0:T(4,128)S(1)}, u32[]{:S(2)}, u32[]{:S(2)}) %collective-permute-start.6) | collective-permute-done | bytes 131104 | tf_op jit(solution)/shard_map/ppermute | solution.py:10
  140.2 2.5 %collective-permute-start.7 = (f32[2,1,1,8,2048]{4,3,2,0,1:T(8,128)}, f32[2,1,1,8,2048]{4,3,2,0,1:T(8,128)}, u32[]{:S(2)}, u32[]{:S(2)}) collective-permute-start(f32[2,1,1,8,2048]{4,3,2,0,1:T(8,128)} %dynamic-slice_select_fusion), channel_id=1, source_target_pairs={{0,512},{64,576},{128,640},{192,704},{256,768},{320,832},{384,896}... | collective-permute-start | bytes 393224 | tf_op jit(solution)/shard_map/ppermute | solution.py:10
  143.5 1.4 broadcast_in_dim.246
  144.9 1.4 broadcast_in_dim.251
  146.3 2.6 %collective-permute-done.7 = f32[2,1,1,8,2048]{4,3,2,0,1:T(8,128)} collective-permute-done((f32[2,1,1,8,2048]{4,3,2,0,1:T(8,128)}, f32[2,1,1,8,2048]{4,3,2,0,1:T(8,128)}, u32[]{:S(2)}, u32[]{:S(2)}) %collective-permute-start.7) | collective-permute-done | bytes 131104 | tf_op jit(solution)/shard_map/ppermute | solution.py:10
  149.9 1.3 broadcast_in_dim.257
  151.2 2.2 %select_select_fusion = f32[2,16,64,32]{3,2,1,0:T(8,128)S(1)} fusion(f32[2,16,64,32]{3,2,1,0:T(8,128)} %broadcast_in_dim.257, f32[2,16,64,32]{3,2,1,0:T(8,128)} %broadcast_in_dim.251, f32[2,16,64,32]{3,2,1,0:T(8,128)} %broadcast_in_dim.246, f32[2,16,64,32]{3,2,1,0:T(8,128)S(1)} %reshape_reshape.53, f32[2,16,64,32]{3,2,1,0:T(8,128)S(1)} %broadcast_in_dim.243, ...), kind=kLoop, calls=%fused_computation.6 | loop fusion | flops 262144 | bytes 1572928 | tf_op jit(solution)/shard_map/jit(_where)/select_n | solution.py:35
  154.1 1.2 reshape.290
  155.2 4.6 %all-to-all-start.1 = ((f32[64,1,1024]{2,1,0:T(1,128)}), f32[64,1,1024]{2,1,0:T(1,128)S(1)}, u32[]{:S(2)}, u32[]{:S(2)}) async-start(f32[64,1,1024]{2,1,0:T(1,128)} %reshape.290), calls=%async_computation.1 | async-start | bytes 524288 | tf_op jit(solution)/shard_map/all_to_all | solution.py:43
  159.9 39.8 %all-to-all-done.1 = f32[64,1,1024]{2,1,0:T(1,128)S(1)} async-done(((f32[64,1,1024]{2,1,0:T(1,128)}), f32[64,1,1024]{2,1,0:T(1,128)S(1)}, u32[]{:S(2)}, u32[]{:S(2)}) %all-to-all-start.1) | async-done | bytes 262176 | tf_op jit(solution)/shard_map/all_to_all | solution.py:43
  199.7 1.2 reduce.3
  (136 shorter events, 23.5 us)
Async XLA Ops:
  0.0 2.0 copy-start
  2.6 0.9 copy-start.7
  5.0 3.2 %collective-permute-start = (f32[2,8,1,1,2048]{4,2,1,0,3:T(1,128)S(1)}, f32[2,8,1,1,2048]{4,2,1,0,3:T(1,128)S(1)}, u32[]{:S(2)}, u32[]{:S(2)}) collective-permute-start(f32[2,8,1,1,2048]{4,2,1,0,3:T(1,128)S(1)} %constant_dynamic-slice_fusion.3), channel_id=1, source_target_pairs={{0,64},{64,0},{128,192},{192,128},{256,320},{320,256},{384,448},{4... | collective-permute-start | bytes 393224 | tf_op jit(solution)/shard_map/ppermute | solution.py:10
  8.8 8.9 %collective-permute-start.1 = (f32[2,4,1,2,2048]{4,3,2,1,0:T(2,128)S(1)}, f32[2,4,1,2,2048]{4,3,2,1,0:T(2,128)S(1)}, u32[]{:S(2)}, u32[]{:S(2)}) collective-permute-start(f32[2,4,1,2,2048]{4,3,2,1,0:T(2,128)S(1)} %dynamic-slice_select_fusion.11), channel_id=1, source_target_pairs={{0,128},{64,192},{128,0},{192,64},{256,384},{320,448},{384,256},{4... | collective-permute-start | bytes 393224 | tf_op jit(solution)/shard_map/ppermute | solution.py:10
  18.2 6.9 %collective-permute-start.2 = (f32[2,2,1,4,2048]{4,3,2,1,0:T(4,128)S(1)}, f32[2,2,1,4,2048]{4,3,2,1,0:T(4,128)S(1)}, u32[]{:S(2)}, u32[]{:S(2)}) collective-permute-start(f32[2,2,1,4,2048]{4,3,2,1,0:T(4,128)S(1)} %dynamic-slice_select_fusion.9), channel_id=1, source_target_pairs={{0,256},{64,320},{128,384},{192,448},{256,0},{320,64},{384,128},{4... | collective-permute-start | bytes 393224 | tf_op jit(solution)/shard_map/ppermute | solution.py:10
  21.9 9.9 %copy-start.8 = (pred[8]{0:T(512)(128)(4,1)}, pred[8]{0:T(512)(128)(4,1)S(1)}, u32[]{:S(2)}) copy-start(pred[8]{0:T(512)(128)(4,1)S(1)} %broadcast_in_dim.207) | copy-start | bytes 28
  22.1 10.4 %copy-start.10 = (pred[8]{0:T(512)(128)(4,1)}, pred[8]{0:T(512)(128)(4,1)S(1)}, u32[]{:S(2)}) copy-start(pred[8]{0:T(512)(128)(4,1)S(1)} %broadcast_in_dim.200) | copy-start | bytes 28
  26.0 11.1 %collective-permute-start.3 = (f32[2,1,1,8,2048]{4,3,2,0,1:T(8,128)}, f32[2,1,1,8,2048]{4,3,2,0,1:T(8,128)}, u32[]{:S(2)}, u32[]{:S(2)}) collective-permute-start(f32[2,1,1,8,2048]{4,3,2,0,1:T(8,128)} %dynamic-slice_select_fusion.6), channel_id=1, source_target_pairs={{0,512},{64,576},{128,640},{192,704},{256,768},{320,832},{384,896}... | collective-permute-start | bytes 393224 | tf_op jit(solution)/shard_map/ppermute | solution.py:10
  38.0 1.4 copy-start.12
  38.0 1.4 copy-start.14
  38.0 1.4 copy-start.16
  38.0 1.4 copy-start.18
  43.4 30.5 %copy-start.1 = (f32[1,128,128]{2,1,0:T(8,128)S(1)}, f32[1,128,128]{2,1,0:T(8,128)}, u32[]{:S(2)}) copy-start(f32[1,128,128]{2,1,0:T(8,128)} %get-tuple-element.14) | copy-start | bytes 196612
  43.4 30.5 %copy-start.2 = (f32[1,128,128]{2,1,0:T(8,128)S(1)}, f32[1,128,128]{2,1,0:T(8,128)}, u32[]{:S(2)}) copy-start(f32[1,128,128]{2,1,0:T(8,128)} %get-tuple-element.15) | copy-start | bytes 196612
  43.4 30.6 %copy-start.3 = (f32[1,128,128]{2,1,0:T(8,128)S(1)}, f32[1,128,128]{2,1,0:T(8,128)}, u32[]{:S(2)}) copy-start(f32[1,128,128]{2,1,0:T(8,128)} %get-tuple-element.16) | copy-start | bytes 196612
  43.4 30.6 %copy-start.4 = (f32[1,128,128]{2,1,0:T(8,128)S(1)}, f32[1,128,128]{2,1,0:T(8,128)}, u32[]{:S(2)}) copy-start(f32[1,128,128]{2,1,0:T(8,128)} %get-tuple-element.17) | copy-start | bytes 196612
  43.4 30.6 %copy-start.5 = (f32[1,128,128]{2,1,0:T(8,128)S(1)}, f32[1,128,128]{2,1,0:T(8,128)}, u32[]{:S(2)}) copy-start(f32[1,128,128]{2,1,0:T(8,128)} %get-tuple-element.8) | copy-start | bytes 196612
  43.4 30.6 %copy-start.6 = (f32[1,128,128]{2,1,0:T(8,128)S(1)}, f32[1,128,128]{2,1,0:T(8,128)}, u32[]{:S(2)}) copy-start(f32[1,128,128]{2,1,0:T(8,128)} %get-tuple-element.9) | copy-start | bytes 196612
  43.4 70.9 %all-to-all-start = ((f32[64,1,1024]{2,1,0:T(1,128)}), f32[64,1,1024]{2,1,0:T(1,128)S(1)}, u32[]{:S(2)}, u32[]{:S(2)}) async-start(f32[64,1,1024]{2,1,0:T(1,128)} %reshape.288), calls=%async_computation | async-start | bytes 524288 | tf_op jit(solution)/shard_map/all_to_all | solution.py:43
  118.6 3.2 %collective-permute-start.4 = (f32[2,8,1,1,2048]{4,2,1,0,3:T(1,128)S(1)}, f32[2,8,1,1,2048]{4,2,1,0,3:T(1,128)S(1)}, u32[]{:S(2)}, u32[]{:S(2)}) collective-permute-start(f32[2,8,1,1,2048]{4,2,1,0,3:T(1,128)S(1)} %constant_dynamic-slice_fusion.1), channel_id=1, source_target_pairs={{0,64},{64,0},{128,192},{192,128},{256,320},{320,256},{384,448},{4... | collective-permute-start | bytes 393224 | tf_op jit(solution)/shard_map/ppermute | solution.py:10
  122.5 8.9 %collective-permute-start.5 = (f32[2,4,1,2,2048]{4,3,2,1,0:T(2,128)S(1)}, f32[2,4,1,2,2048]{4,3,2,1,0:T(2,128)S(1)}, u32[]{:S(2)}, u32[]{:S(2)}) collective-permute-start(f32[2,4,1,2,2048]{4,3,2,1,0:T(2,128)S(1)} %dynamic-slice_select_fusion.5), channel_id=1, source_target_pairs={{0,128},{64,192},{128,0},{192,64},{256,384},{320,448},{384,256},{4... | collective-permute-start | bytes 393224 | tf_op jit(solution)/shard_map/ppermute | solution.py:10
  131.9 6.9 %collective-permute-start.6 = (f32[2,2,1,4,2048]{4,3,2,1,0:T(4,128)S(1)}, f32[2,2,1,4,2048]{4,3,2,1,0:T(4,128)S(1)}, u32[]{:S(2)}, u32[]{:S(2)}) collective-permute-start(f32[2,2,1,4,2048]{4,3,2,1,0:T(4,128)S(1)} %dynamic-slice_select_fusion.3), channel_id=1, source_target_pairs={{0,256},{64,320},{128,384},{192,448},{256,0},{320,64},{384,128},{4... | collective-permute-start | bytes 393224 | tf_op jit(solution)/shard_map/ppermute | solution.py:10
  138.8 0.7 copy-start.9
  138.8 0.7 copy-start.11
  140.2 8.7 %collective-permute-start.7 = (f32[2,1,1,8,2048]{4,3,2,0,1:T(8,128)}, f32[2,1,1,8,2048]{4,3,2,0,1:T(8,128)}, u32[]{:S(2)}, u32[]{:S(2)}) collective-permute-start(f32[2,1,1,8,2048]{4,3,2,0,1:T(8,128)} %dynamic-slice_select_fusion), channel_id=1, source_target_pairs={{0,512},{64,576},{128,640},{192,704},{256,768},{320,832},{384,896}... | collective-permute-start | bytes 393224 | tf_op jit(solution)/shard_map/ppermute | solution.py:10
  149.8 1.4 copy-start.13
  149.8 1.4 copy-start.15
  149.8 1.4 copy-start.17
  149.8 1.4 copy-start.19
  155.2 44.5 %all-to-all-start.1 = ((f32[64,1,1024]{2,1,0:T(1,128)}), f32[64,1,1024]{2,1,0:T(1,128)S(1)}, u32[]{:S(2)}, u32[]{:S(2)}) async-start(f32[64,1,1024]{2,1,0:T(1,128)} %reshape.290), calls=%async_computation.1 | async-start | bytes 524288 | tf_op jit(solution)/shard_map/all_to_all | solution.py:43
where the time goes:
time: 205 us; the launch traced here: 204 us
  waiting for transfers between devices  102 us (50%)
  starting transfers between devices  58.7 us (29%)
  local copies, waits for them, and re-layouts  30.4 us (15%)
  other arithmetic  10.2 us (5%)
  matrix products  2.26 us (1%)
    all_to_all x2, waiting for transfers between devices, remap_narrow(): lax.all_to_all(shaped, 'narrow', split_axis=2, concat_axis=2, tiled=True)  80.1 us
    all_to_all x2, starting transfers between devices, remap_narrow(): lax.all_to_all(shaped, 'narrow', split_axis=2, concat_axis=2, tiled=True)  35.1 us
    ppermute x8, starting transfers between devices, from_partner(): return lax.ppermute(value, axis, pairs)  23.6 us
    ppermute x8, waiting for transfers between devices, from_partner(): return lax.ppermute(value, axis, pairs)  21.7 us
    broadcast_in_dim x46, local copies, waits for them, and re-layouts, remap_wide(): jnp.where(marker == own_bit, shaped, arrived).reshape(amplitudes.shape)  16.7 us
    select_n x8, other arithmetic, remap_wide(): jnp.where(marker == own_bit, shaped, arrived).reshape(amplitudes.shape)  6.45 us
    unnamed x45, local copies, waits for them, and re-layouts  5.44 us
  transfers between devices with their start and end apart: 10, of which 9 were waited for; matrix products, arithmetic and copies ran while one was open for 6% of the time, Pallas kernels for 0%

commit v1 on v0

v1 whole, which is shorter than its diff:
```python
import jax
import jax.numpy as jnp
from jax import lax
from jax.sharding import PartitionSpec as P

AXES = ("wide", "narrow")


def apply_layer(x, u, v):
    um = jnp.stack([jnp.stack([u[0], -u[1]]), jnp.stack([u[1], u[0]])])
    vm = jnp.stack([jnp.stack([v[0], -v[1]]), jnp.stack([v[1], v[0]])])
    y = jnp.einsum("kcji,ciqs->ksjq", um, x, precision=lax.Precision.HIGHEST)
    return jnp.einsum("ksjq,mkpq->msjp", y, vm, precision=lax.Precision.HIGHEST)


def remap(x):
    blocks = lax.axis_size("wide") * lax.axis_size("narrow")
    shaped = x.reshape(2, blocks, -1).transpose(1, 0, 2)
    moved = lax.all_to_all(shaped, AXES, split_axis=0, concat_axis=0, tiled=True)
    return moved.transpose(1, 0, 2).reshape(2, -1)


def on_device(state, gates):
    x = state
    layers = gates.shape[0] // 2
    dim = gates.shape[-1]
    for l in range(layers):
        y = apply_layer(x.reshape(2, dim, dim, -1), gates[2 * l], gates[2 * l + 1])
        x = y.reshape(2, -1)
        if l + 1 < layers:
            x = remap(x)
    return x


def solution(mesh):
    return jax.shard_map(
        on_device,
        mesh=mesh,
        in_specs=(P(None, AXES), P()),
        out_specs=P(None, AXES),
        check_vma=False,
    )
```

time: 205 us -> 365 us (1.78)
  blocking collectives: 0 us -> 125 us
  local copies, waits for them, and re-layouts: 30.4 us -> 87 us
  starting transfers between devices: 58.7 us -> 40.4 us
  other arithmetic: 10.2 us -> 1.15 us
  waiting for transfers between devices: 102 us -> 108 us
    all_to_all x0 -> x1, blocking collectives: none -> 125 us  [remap(): lax.all_to_all(shaped, AXES, split_axis=0, concat_axis=0, tiled=True)]
    another operation x15 -> x6, local copies, waits for them, and re-layouts: 2.21 us -> 46.9 us  [the longest x4 46.4 us: on_device(): y = apply_layer(x.reshape(2, dim, dim, -1), gates[2 * l], gates[2 * l + 1])]
    reshape x0 -> x2, local copies, waits for them, and re-layouts: none -> 34.8 us  [on_device(): y = apply_layer(x.reshape(2, dim, dim, -1), gates[2 * l], gates[2 * l + 1])]
    all_to_all x2 -> x1, waiting for transfers between devices: 80.1 us -> 108 us  [remap(): lax.all_to_all(shaped, AXES, split_axis=0, concat_axis=0, tiled=True)]
    ppermute x8 -> x0, starting transfers between devices: 23.6 us -> none  [from_partner(): return lax.ppermute(value, axis, pairs)]
    ppermute x8 -> x0, waiting for transfers between devices: 21.7 us -> none  [from_partner(): return lax.ppermute(value, axis, pairs)]
    broadcast_in_dim x46 -> x0, local copies, waits for them, and re-layouts: 16.7 us -> none  [remap_wide(): jnp.where(marker == own_bit, shaped, arrived).reshape(amplitudes.shape)]
    select_n x8 -> x0, other arithmetic: 6.45 us -> none  [remap_wide(): jnp.where(marker == own_bit, shaped, arrived).reshape(amplitudes.shape)]
  transfers between devices with their start and end apart: 10 -> 1, of which waited for: 9 -> 1; matrix products, arithmetic and copies ran while one was open for 6% -> 0% of each run, Pallas kernels for 0% -> 0%
where the time goes in v1:
time: 365 us; the launch traced here: 364 us
  blocking collectives  125 us (34%)
  waiting for transfers between devices  108 us (30%)
  local copies, waits for them, and re-layouts  87 us (24%)
  starting transfers between devices  40.4 us (11%)
    all_to_all x1, blocking collectives, remap(): lax.all_to_all(shaped, AXES, split_axis=0, concat_axis=0, tiled=True)  125 us
    all_to_all x1, waiting for transfers between devices, remap(): lax.all_to_all(shaped, AXES, split_axis=0, concat_axis=0, tiled=True)  108 us
    another operation x4, local copies, waits for them, and re-layouts, on_device(): y = apply_layer(x.reshape(2, dim, dim, -1), gates[2 * l], gates[2 * l + 1])  46.4 us
    all_to_all x1, starting transfers between devices, remap(): lax.all_to_all(shaped, AXES, split_axis=0, concat_axis=0, tiled=True)  40.4 us
    reshape x2, local copies, waits for them, and re-layouts, on_device(): y = apply_layer(x.reshape(2, dim, dim, -1), gates[2 * l], gates[2 * l + 1])  34.8 us
  transfers between devices with their start and end apart: 1, of which 1 were waited for; matrix products, arithmetic and copies ran while one was open for 0% of the time, Pallas kernels for 0%

profile of v1, /device:TPU:24, one launch (start us, length us, event | category | flops | bytes accessed | tf_op | source)
XLA Modules:
  0.0 363.8 jit_solution(9754674006700754005)
XLA Ops:
  0.0 1.2 slice_bitcast_fusion.10
  1.2 1.0 fusion.18
  2.2 24.9 %reshape.84 = f32[2,128,128,2]{3,2,1,0:T(8,128)} reshape(f32[2,32768]{1,0:T(2,128)} %param.2) | data formatting | bytes 524288 | tf_op jit(solution)/shard_map/reshape | solution.py:28
  27.1 10.0 %copy.18 = f32[2,128,128,2,1]{2,1,0,4,3:T(8,128)S(1)} copy(f32[2,128,128,2,1]{3,2,1,0,4:T(8,128)} %bitcast.144) | data formatting | bytes 524288 | tf_op jit(solution)/shard_map/reshape | solution.py:28
  37.1 0.4 convolution_bitcast_fusion.5
  37.5 0.4 convolution_bitcast_fusion.4
  37.9 0.1 copy.7
  38.1 0.3 reshape_reshape.12
  38.3 1.8 copy.8
  40.1 40.4 %all-to-all-start = ((f32[1024,2,32]{2,1,0:T(2,128)}), f32[1024,2,32]{2,1,0:T(2,128)S(1)}, u32[]{:S(2)}, u32[]{:S(2)}) async-start(f32[1024,2,32]{2,1,0:T(2,128)} %copy.8), calls=%async_computation | async-start | bytes 2097152 | tf_op jit(solution)/shard_map/all_to_all | solution.py:19
  80.6 108.2 %all-to-all-done = f32[1024,2,32]{2,1,0:T(2,128)S(1)} async-done(((f32[1024,2,32]{2,1,0:T(2,128)}), f32[1024,2,32]{2,1,0:T(2,128)S(1)}, u32[]{:S(2)}, u32[]{:S(2)}) %all-to-all-start) | async-done | bytes 262176 | tf_op jit(solution)/shard_map/all_to_all | solution.py:19
  188.8 0.1 copy.9
  188.8 11.1 %reshape_reshape.13 = f32[2,128,128,2]{3,2,1,0:T(8,128)} reshape(f32[2,1024,32]{2,1,0:T(8,128)S(1)} %copy.9) | data formatting | bytes 524288 | tf_op jit(solution)/shard_map/reshape;reshape | solution.py:28
  199.9 12.1 %copy.22 = f32[2,128,128,2,1]{1,2,0,4,3:T(8,128)S(1)} copy(f32[2,128,128,2,1]{3,2,1,0,4:T(8,128)} %bitcast.142) | data formatting | bytes 524288 | tf_op jit(solution)/shard_map/reshape;reshape | solution.py:28
  212.0 0.4 convolution_bitcast_fusion.3
  212.4 0.4 convolution_bitcast_fusion.2
  212.8 0.1 copy.12
  213.0 0.3 reshape_reshape.14
  213.2 0.8 copy.13
  214.0 124.6 %all_to_all.10 = f32[1024,2,32]{2,1,0:T(2,128)S(1)} all-to-all(f32[1024,2,32]{2,1,0:T(2,128)S(1)} %copy.13), channel_id=1, replica_groups=mesh['wide'=16,'narrow'=64] {'wide','narrow'}, dimensions={0} | all-to-all | bytes 524288 | tf_op jit(solution)/shard_map/all_to_all | solution.py:19
  338.7 0.1 copy.14
  338.7 11.1 %reshape_reshape.15 = f32[2,128,128,2]{3,2,1,0:T(8,128)} reshape(f32[2,1024,32]{2,1,0:T(8,128)S(1)} %copy.14) | data formatting | bytes 524288 | tf_op jit(solution)/shard_map/reshape;reshape | solution.py:28
  349.8 12.1 %copy.27 = f32[2,128,128,2,1]{1,2,0,4,3:T(8,128)S(1)} copy(f32[2,128,128,2,1]{3,2,1,0,4:T(8,128)} %bitcast.143) | data formatting | bytes 524288 | tf_op jit(solution)/shard_map/reshape;reshape | solution.py:28
  361.9 0.4 convolution_bitcast_fusion.1
  362.4 0.4 convolution_bitcast_fusion
  362.7 0.1 copy.17
  362.9 0.9 copy.42
  (3 shorter events, 0.1 us)
Async XLA Ops:
  40.1 148.6 %all-to-all-start = ((f32[1024,2,32]{2,1,0:T(2,128)}), f32[1024,2,32]{2,1,0:T(2,128)S(1)}, u32[]{:S(2)}, u32[]{:S(2)}) async-start(f32[1024,2,32]{2,1,0:T(2,128)} %copy.8), calls=%async_computation | async-start | bytes 2097152 | tf_op jit(solution)/shard_map/all_to_all | solution.py:19

commit v2 on v1

v2 whole, which is shorter than its diff:
```python
import jax
import jax.numpy as jnp
from jax import lax
from jax.experimental import pallas as pl
from jax.experimental.pallas import tpu as pltpu
from jax.sharding import PartitionSpec as P

AXES = ("wide", "narrow")
MESH = pl.DeviceIdType.MESH
NZ = 32
NP = 32


def dot(a, b):
    return lax.dot_general(
        a, b, (((1,), (0,)), ((), ())), precision=lax.Precision.HIGHEST, preferred_element_type=jnp.float32
    )


def dot_nt(a, b):
    return lax.dot_general(
        a, b, (((1,), (1,)), ((), ())), precision=lax.Precision.HIGHEST, preferred_element_type=jnp.float32
    )


def iota(shape, dim):
    return lax.broadcasted_iota(jnp.int32, shape, dim)


def in_parts(k, first):
    if first:
        return (k >> 8) * 64 + ((k >> 1) & 63), k & 1, (k >> 7) & 1
    return (k >> 6) * 16 + ((k >> 1) & 15), k & 1, (k >> 5) & 1


def out_parts(k, last):
    if last:
        return k & 127, (k >> 7) & 1, k >> 8
    return ((k >> 6) & 1) * 64 + ((k >> 7) & 1) * 32 + (k & 31), k >> 8, (k >> 5) & 1


def expand_second(u, first, last):
    i2, _, _ = in_parts(iota((512, 128), 0), first)
    rows = (i2 == iota((512, 128), 1)).astype(jnp.float32)
    j2, _, _ = out_parts(iota((128, 512), 1), last)
    cols = (j2 == iota((128, 512), 0)).astype(jnp.float32)
    real = dot(dot_nt(rows, u[:128]), cols)
    imag = dot(dot_nt(rows, u[128:]), cols)
    _, s_in, c_in = in_parts(iota((512, 512), 0), first)
    _, s_out, c_out = out_parts(iota((512, 512), 1), last)
    full = jnp.where(c_in == c_out, real, jnp.where(c_in < c_out, imag, -imag))
    return jnp.where(s_in == s_out, full, 0.0)


def permute_first(u):
    k = iota((128, 128), 1)
    pick = (iota((128, 128), 0) == (k & 15) * 8 + (k >> 4)).astype(jnp.float32)
    return dot(u, pick)


def times_i(tiles, first, roll):
    if first:
        return [-tiles[1], tiles[0], -tiles[3], tiles[2]]
    real = ((iota((128, 128), 1) >> 5) & 1) == 0
    return [jnp.where(real, -roll(t, 96), roll(t, 32)) for t in tiles]


def layer(tiles, u1, m, first, roll):
    both = [dot(u1, t) for t in tiles]
    turned = times_i([t[128:] for t in both], first, roll)
    z = jnp.concatenate([a[:128] + b for a, b in zip(both, turned)], axis=1)
    return dot(z, m)


def lane_roll(x, by):
    return pltpu.roll(x, by, 1)


def kernel(state, gates, out, s1, r1, s2, r2, mats, firsts, plane_send, plane_recv, z_send, z_recv):
    wide = lax.axis_index("wide")
    narrow = lax.axis_index("narrow")
    z = narrow // 2
    plane = (wide // 8) * 16 + (narrow % 2) * 8 + wide % 8

    def plane_id(p):
        return ((p // 16) * 8 + p % 8, z * 2 + (p // 8) % 2)

    def z_id(other):
        return (wide, other * 2 + narrow % 2)

    def z_slot(other):
        return (other % 4) * 8 + other // 4

    barrier = pltpu.get_barrier_semaphore()

    def greet(k, _):
        pl.semaphore_signal(barrier, inc=1, device_id=z_id((z + k) % NZ), device_id_type=MESH)
        pl.semaphore_signal(barrier, inc=1, device_id=plane_id((plane + k) % NP), device_id_type=MESH)
        return 0

    lax.fori_loop(1, 32, greet, 0)

    def send_plane(o, t):
        for part in range(4):
            s1[t, part * 8 : part * 8 + 8] = o[:, part * 128 : part * 128 + 128].reshape(8, 16, 128)

    def start_plane(t):
        pltpu.make_async_copy(s1.at[t, plane], r1.at[t, plane], plane_recv.at[t]).start()

        def send(k, _):
            p = (plane + k) % NP
            pltpu.make_async_remote_copy(
                src_ref=s1.at[t, p],
                dst_ref=r1.at[t, plane],
                send_sem=plane_send.at[t],
                recv_sem=plane_recv.at[t],
                device_id=plane_id(p),
                device_id_type=MESH,
            ).start()
            return 0

        lax.fori_loop(1, NP, send, 0)

    def wait_plane(t):
        pltpu.make_async_copy(r1.at[t], r1.at[t], plane_recv.at[t]).wait()

    def shuffle(t):
        low = iota((16, 128), 1) < 64
        for w in range(16):
            p = (w // 8) * 16 + w % 8
            a = r1[t, p]
            b = r1[t, p + 8]
            s2[t, pl.ds(w, 16, 32), :] = jnp.where(low, a, lane_roll(b, 64))
            s2[t, pl.ds(16 + w, 16, 32), :] = jnp.where(low, lane_roll(a, 64), b)

    def start_z(t):
        def copy(other):
            return pltpu.make_async_remote_copy(
                src_ref=s2.at[t, pl.ds(pl.multiple_of(other * 16, 16), 16)],
                dst_ref=r2.at[t, z_slot(z)],
                send_sem=z_send.at[t],
                recv_sem=z_recv.at[t],
                device_id=z_id(other),
                device_id_type=MESH,
            )

        copy((z + 16) % NZ).start()

        def send(k, _):
            copy((z + 16 - k) % NZ).start()
            copy((z + 16 + k) % NZ).start()
            return 0

        lax.fori_loop(1, 16, send, 0)
        pltpu.make_async_copy(
            s2.at[t, pl.ds(pl.multiple_of(z * 16, 16), 16)], r2.at[t, z_slot(z)], z_recv.at[t]
        ).start()

    def wait_z(t):
        pltpu.make_async_copy(r2.at[t], r2.at[t], z_recv.at[t]).wait()

    def prepare(l):
        mats[l] = expand_second(gates[2 * l + 1], l == 0, l == 2)
        if l > 0:
            firsts[l - 1] = permute_first(gates[2 * l])

    prepare(0)
    tiles = [state[pl.ds(q, 128, 4), :] for q in range(4)]
    o = layer(tiles, gates[0], mats[0], True, lane_roll)
    for l in range(1, 3):
        t = l - 1
        send_plane(o, t)
        if l == 1:
            pl.semaphore_wait(barrier, 62)
        start_plane(t)
        wait_plane(t)
        shuffle(t)
        start_z(t)
        prepare(l)
        wait_z(t)
        tiles = [r2[t, q * 8 : q * 8 + 8].reshape(128, 128) for q in range(4)]
        o = layer(tiles, firsts[t], mats[l], False, lane_roll)
    for c in range(2):
        for s in range(2):
            q = c * 2 + s
            out[pl.ds(s * 256 + c, 128, 2), :] = o[:, q * 128 : q * 128 + 128]
    for t in range(2):
        pltpu.make_async_copy(s1.at[t, pl.ds(0, 31)], s1.at[t, pl.ds(0, 31)], plane_send.at[t]).wait()
        pltpu.make_async_copy(s2.at[t, pl.ds(0, 496)], s2.at[t, pl.ds(0, 496)], z_send.at[t]).wait()


def on_device(state, gates):
    rows = state.reshape(2, 256, 128).transpose(1, 0, 2).reshape(512, 128)
    vmem = pl.BlockSpec(memory_space=pltpu.VMEM)
    out = pl.pallas_call(
        kernel,
        out_shape=jax.ShapeDtypeStruct((512, 128), jnp.float32),
        in_specs=[vmem, vmem],
        out_specs=vmem,
        scratch_shapes=[
            pltpu.VMEM((2, NP, 16, 128), jnp.float32),
            pltpu.VMEM((2, NP, 16, 128), jnp.float32),
            pltpu.VMEM((2, NZ * 16, 128), jnp.float32),
            pltpu.VMEM((2, NZ, 16, 128), jnp.float32),
            pltpu.VMEM((3, 512, 512), jnp.float32),
            pltpu.VMEM((2, 256, 128), jnp.float32),
            pltpu.SemaphoreType.DMA((2,)),
            pltpu.SemaphoreType.DMA((2,)),
            pltpu.SemaphoreType.DMA((2,)),
            pltpu.SemaphoreType.DMA((2,)),
        ],
        compiler_params=pltpu.CompilerParams(collective_id=0, has_side_effects=True),
        name="window",
    )(rows, gates.reshape(6, 256, 128))
    return out.reshape(256, 2, 128).transpose(1, 0, 2).reshape(2, 32768)


def solution(mesh):
    return jax.shard_map(
        on_device,
        mesh=mesh,
        in_specs=(P(None, AXES), P()),
        out_specs=P(None, AXES),
        check_vma=False,
    )
```

time: 365 us -> 99.6 us (0.27)
  blocking collectives: 125 us -> 0 us
  waiting for transfers between devices: 108 us -> 0 us
  Pallas kernels: 0 us -> 97.3 us
  local copies, waits for them, and re-layouts: 87 us -> 1.67 us
  starting transfers between devices: 40.4 us -> 0 us
    all_to_all x1 -> x0, blocking collectives: 125 us -> none  [remap(): lax.all_to_all(shaped, AXES, split_axis=0, concat_axis=0, tiled=True)]
    all_to_all x1 -> x0, waiting for transfers between devices: 108 us -> none  [remap(): lax.all_to_all(shaped, AXES, split_axis=0, concat_axis=0, tiled=True)]
    pallas_call x0 -> x1, Pallas kernels: none -> 97.3 us  [on_device(): pl.pallas_call(kernel, out_shape=jax.ShapeDtypeStruct((512, 128), jnp.flo...]
    another operation x6 -> x0, local copies, waits for them, and re-layouts: 46.9 us -> none  [the longest x4 46.4 us: on_device(): y = apply_layer(x.reshape(2, dim, dim, -1), gates[2 * l], gates[2 * l + 1])]
    all_to_all x1 -> x0, starting transfers between devices: 40.4 us -> none  [remap(): lax.all_to_all(shaped, AXES, split_axis=0, concat_axis=0, tiled=True)]
    reshape x2 -> x0, local copies, waits for them, and re-layouts: 34.8 us -> none  [on_device(): y = apply_layer(x.reshape(2, dim, dim, -1), gates[2 * l], gates[2 * l + 1])]
  transfers between devices with their start and end apart: 1 -> 0, of which waited for: 1 -> 0; matrix products, arithmetic and copies ran while one was open for 0% -> 0% of each run, Pallas kernels for 0% -> 0%
where the time goes in v2:
time: 99.6 us; the launch traced here: 99 us
  Pallas kernels  97.3 us (98%)
  local copies, waits for them, and re-layouts  1.67 us (2%)
    pallas_call x1, Pallas kernels, on_device(): pl.pallas_call(kernel, out_shape=jax.ShapeDtypeStruct((512, 128), jnp.flo...  97.3 us

profile of v2, /device:TPU:24, one launch (start us, length us, event | category | flops | bytes accessed | tf_op | source)
XLA Modules:
  0.0 99.0 jit_solution(12708936172630936739)
XLA Ops:
  0.0 97.3 %window.1 = f32[512,128]{1,0:T(8,128)} custom-call(f32[512,128]{1,0:T(8,128)} %bitcast.13, f32[6,256,128]{2,1,0:T(8,128)} %bitcast.12), custom_call_target="tpu_custom_call" | custom-call | tf_op jit(solution)/shard_map/window/pallas_call | solution.py:195
  97.3 1.7 %copy.6 = f32[2,32768]{1,0:T(2,128)} copy(f32[2,32768]{1,0:T(2,128)} %bitcast.11) | data formatting | bytes 524288

commit v3 on v2

--- a/solution.py
+++ b/solution.py
@@ -76,10 +76,12 @@
     return pltpu.roll(x, by, 1)
 
 
-def kernel(state, gates, out, s1, r1, s2, r2, mats, firsts, plane_send, plane_recv, z_send, z_recv):
+def kernel(state_hbm, gates_hbm, out, state, gates, s1, r1, s2, r2, mats, firsts, *sems):
+    load, plane_send, plane_recv, z_send, z_recv, relay = sems
     wide = lax.axis_index("wide")
     narrow = lax.axis_index("narrow")
     z = narrow // 2
+    mine = z // 16
     plane = (wide // 8) * 16 + (narrow % 2) * 8 + wide % 8
 
     def plane_id(p):
@@ -91,29 +93,46 @@
     def z_slot(other):
         return (other % 4) * 8 + other // 4
 
+    def signal_z(sem, step):
+        for other in ((z + step) % NZ, (z + NZ - step) % NZ):
+            pl.semaphore_signal(sem, inc=1, device_id=z_id(other), device_id_type=MESH)
+
     barrier = pltpu.get_barrier_semaphore()
 
     def greet(k, _):
-        pl.semaphore_signal(barrier, inc=1, device_id=z_id((z + k) % NZ), device_id_type=MESH)
         pl.semaphore_signal(barrier, inc=1, device_id=plane_id((plane + k) % NP), device_id_type=MESH)
         return 0
 
-    lax.fori_loop(1, 32, greet, 0)
-
-    def send_plane(o, t):
+    signal_z(barrier, 1)
+    lax.fori_loop(1, NP, greet, 0)
+    loads = [
+        pltpu.make_async_copy(gates_hbm.at[pl.ds(0, 2)], gates.at[pl.ds(0, 2)], load.at[0]),
+        pltpu.make_async_copy(state_hbm, state, load.at[1]),
+        pltpu.make_async_copy(gates_hbm.at[pl.ds(2, 4)], gates.at[pl.ds(2, 4)], load.at[2]),
+    ]
+    for copy in loads:
+        copy.start()
+
+    def half(phase):
+        return 1 - mine if phase == 0 else mine
+
+    def place(o, t):
         for part in range(4):
-            s1[t, part * 8 : part * 8 + 8] = o[:, part * 128 : part * 128 + 128].reshape(8, 16, 128)
-
-    def start_plane(t):
-        pltpu.make_async_copy(s1.at[t, plane], r1.at[t, plane], plane_recv.at[t]).start()
+            tile = o[:, part * 128 : part * 128 + 128].reshape(8, 2, 8, 128)
+            for h in range(2):
+                s1[t, h, part * 8 : part * 8 + 8] = tile[:, h]
+
+    def start_plane(t, phase):
+        h = half(phase)
+        pltpu.make_async_copy(s1.at[t, h, plane], r1.at[t, h, plane], plane_recv.at[t, phase]).start()
 
         def send(k, _):
             p = (plane + k) % NP
             pltpu.make_async_remote_copy(
-                src_ref=s1.at[t, p],
-                dst_ref=r1.at[t, plane],
+                src_ref=s1.at[t, h, p],
+                dst_ref=r1.at[t, h, plane],
                 send_sem=plane_send.at[t],
-                recv_sem=plane_recv.at[t],
+                recv_sem=plane_recv.at[t, phase],
                 device_id=plane_id(p),
                 device_id_type=MESH,
             ).start()
@@ -121,40 +140,49 @@
 
         lax.fori_loop(1, NP, send, 0)
 
-    def wait_plane(t):
-        pltpu.make_async_copy(r1.at[t], r1.at[t], plane_recv.at[t]).wait()
-
-    def shuffle(t):
-        low = iota((16, 128), 1) < 64
+    def wait_plane(t, phase):
+        h = half(phase)
+        pltpu.make_async_copy(r1.at[t, h], r1.at[t, h], plane_recv.at[t, phase]).wait()
+
+    def shuffle(t, phase):
+        h = half(phase)
+        low = iota((8, 128), 1) < 64
         for w in range(16):
             p = (w // 8) * 16 + w % 8
-            a = r1[t, p]
-            b = r1[t, p + 8]
-            s2[t, pl.ds(w, 16, 32), :] = jnp.where(low, a, lane_roll(b, 64))
-            s2[t, pl.ds(16 + w, 16, 32), :] = jnp.where(low, lane_roll(a, 64), b)
-
-    def start_z(t):
-        def copy(other):
-            return pltpu.make_async_remote_copy(
-                src_ref=s2.at[t, pl.ds(pl.multiple_of(other * 16, 16), 16)],
+            a = r1[t, h, p]
+            b = r1[t, h, p + 8]
+            s2[t, h, pl.ds(w, 8, 32), :] = jnp.where(low, a, lane_roll(b, 64))
+            s2[t, h, pl.ds(16 + w, 8, 32), :] = jnp.where(low, lane_roll(a, 64), b)
+
+    def start_z(t, phase):
+        h = half(phase)
+
+        def block(j):
+            return s2.at[t, h, pl.ds(pl.multiple_of(j * 16, 16), 16)]
+
+        def send(k, _):
+            j = (z + k) % 16
+            pltpu.make_async_remote_copy(
+                src_ref=block(j),
                 dst_ref=r2.at[t, z_slot(z)],
                 send_sem=z_send.at[t],
                 recv_sem=z_recv.at[t],
-                device_id=z_id(other),
+                device_id=z_id(h * 16 + j),
                 device_id_type=MESH,
-            )
-
-        copy((z + 16) % NZ).start()
-
-        def send(k, _):
-            copy((z + 16 - k) % NZ).start()
-            copy((z + 16 + k) % NZ).start()
+            ).start()
             return 0
 
-        lax.fori_loop(1, 16, send, 0)
-        pltpu.make_async_copy(
-            s2.at[t, pl.ds(pl.multiple_of(z * 16, 16), 16)], r2.at[t, z_slot(z)], z_recv.at[t]
-        ).start()
+        if phase == 0:
+            send(0, 0)
+        else:
+            pltpu.make_async_copy(block(z % 16), r2.at[t, z_slot(z)], z_recv.at[t]).start()
+
+        def pair(k, _):
+            send(k, 0)
+            return send(16 - k, 0)
+
+        lax.fori_loop(1, 8, pair, 0)
+        send(8, 0)
 
     def wait_z(t):
         pltpu.make_async_copy(r2.at[t], r2.at[t], z_recv.at[t]).wait()
@@ -164,18 +192,28 @@
         if l > 0:
             firsts[l - 1] = permute_first(gates[2 * l])
 
+    loads[0].wait()
     prepare(0)
+    pl.semaphore_wait(barrier, 33)
+    signal_z(relay.at[0], 1)
+    loads[1].wait()
+    loads[2].wait()
     tiles = [state[pl.ds(q, 128, 4), :] for q in range(4)]
     o = layer(tiles, gates[0], mats[0], True, lane_roll)
     for l in range(1, 3):
         t = l - 1
-        send_plane(o, t)
+        place(o, t)
+        start_plane(t, 0)
+        start_plane(t, 1)
         if l == 1:
-            pl.semaphore_wait(barrier, 62)
-        start_plane(t)
-        wait_plane(t)
-        shuffle(t)
-        start_z(t)
+            for step in range(4):
+                pl.semaphore_wait(relay.at[step], 2)
+                if step < 3:
+                    signal_z(relay.at[step + 1], 2 << step)
+        for phase in range(2):
+            wait_plane(t, phase)
+            shuffle(t, phase)
+            start_z(t, phase)
         prepare(l)
         wait_z(t)
         tiles = [r2[t, q * 8 : q * 8 + 8].reshape(128, 128) for q in range(4)]
@@ -184,30 +222,35 @@
         for s in range(2):
             q = c * 2 + s
             out[pl.ds(s * 256 + c, 128, 2), :] = o[:, q * 128 : q * 128 + 128]
+    done = s2.at[0, :, pl.ds(0, 248)]
     for t in range(2):
-        pltpu.make_async_copy(s1.at[t, pl.ds(0, 31)], s1.at[t, pl.ds(0, 31)], plane_send.at[t]).wait()
-        pltpu.make_async_copy(s2.at[t, pl.ds(0, 496)], s2.at[t, pl.ds(0, 496)], z_send.at[t]).wait()
+        for sem in (plane_send, z_send):
+            pltpu.make_async_copy(done, done, sem.at[t]).wait()
 
 
 def on_device(state, gates):
     rows = state.reshape(2, 256, 128).transpose(1, 0, 2).reshape(512, 128)
-    vmem = pl.BlockSpec(memory_space=pltpu.VMEM)
+    hbm = pl.BlockSpec(memory_space=pl.ANY)
     out = pl.pallas_call(
         kernel,
-        out_shape=jax.ShapeDtypeStruct((512, 128), jnp.float32),
-        in_specs=[vmem, vmem],
-        out_specs=vmem,
+        out_shape=pltpu.VMEM((512, 128), jnp.float32),
+        in_specs=[hbm, hbm],
+        out_specs=pl.BlockSpec(memory_space=pltpu.VMEM),
         scratch_shapes=[
-            pltpu.VMEM((2, NP, 16, 128), jnp.float32),
-            pltpu.VMEM((2, NP, 16, 128), jnp.float32),
-            pltpu.VMEM((2, NZ * 16, 128), jnp.float32),
+            pltpu.VMEM((512, 128), jnp.float32),
+            pltpu.VMEM((6, 256, 128), jnp.float32),
+            pltpu.VMEM((2, 2, NP, 8, 128), jnp.float32),
+            pltpu.VMEM((2, 2, NP, 8, 128), jnp.float32),
+            pltpu.VMEM((2, 2, NZ * 8, 128), jnp.float32),
             pltpu.VMEM((2, NZ, 16, 128), jnp.float32),
             pltpu.VMEM((3, 512, 512), jnp.float32),
             pltpu.VMEM((2, 256, 128), jnp.float32),
+            pltpu.SemaphoreType.DMA((3,)),
+            pltpu.SemaphoreType.DMA((2,)),
+            pltpu.SemaphoreType.DMA((2, 2)),
             pltpu.SemaphoreType.DMA((2,)),
             pltpu.SemaphoreType.DMA((2,)),
-            pltpu.SemaphoreType.DMA((2,)),
-            pltpu.SemaphoreType.DMA((2,)),
+            pltpu.SemaphoreType.REGULAR((4,)),
         ],
         compiler_params=pltpu.CompilerParams(collective_id=0, has_side_effects=True),
         name="window",

time: 99.6 us -> 102 us (1.024)
  Pallas kernels: 97.3 us -> 99.7 us
    pallas_call x1, Pallas kernels: 97.3 us -> 99.7 us  [on_device(): pl.pallas_call(kernel, out_shape=pltpu.VMEM((512, 128), jnp.float32), in_...]
where the time goes in v3:
time: 102 us; the launch traced here: 100 us
  Pallas kernels  99.7 us (98%)
    pallas_call x1, Pallas kernels, on_device(): pl.pallas_call(kernel, out_shape=pltpu.VMEM((512, 128), jnp.float32), in_...  99.7 us

profile of v3, /device:TPU:24, one launch (start us, length us, event | category | flops | bytes accessed | tf_op | source)
XLA Modules:
  0.0 100.4 jit_solution(16173527312588568104)
XLA Ops:
  0.0 99.7 %window.1 = f32[512,128]{1,0:T(8,128)S(1)} custom-call(f32[512,128]{1,0:T(8,128)} %bitcast.13, f32[6,256,128]{2,1,0:T(8,128)} %bitcast.12), custom_call_target="tpu_custom_call" | custom-call | tf_op jit(solution)/shard_map/window/pallas_call | solution.py:234
  99.7 0.7 copy.6

commit v4 on v1

v4 whole, which is shorter than its diff:
```python
import jax
import jax.numpy as jnp
from jax import lax
from jax.experimental import pallas as pl
from jax.experimental.pallas import tpu as pltpu
from jax.sharding import PartitionSpec as P

AXES = ("wide", "narrow")
MESH = pl.DeviceIdType.MESH
NZ = 32
NP = 32


def dot(a, b):
    return lax.dot_general(
        a, b, (((1,), (0,)), ((), ())), precision=lax.Precision.HIGHEST, preferred_element_type=jnp.float32
    )


def dot_nt(a, b):
    return lax.dot_general(
        a, b, (((1,), (1,)), ((), ())), precision=lax.Precision.HIGHEST, preferred_element_type=jnp.float32
    )


def iota(shape, dim):
    return lax.broadcasted_iota(jnp.int32, shape, dim)


def in_parts(k, l):
    if l == 0:
        return (k >> 8) * 64 + ((k >> 1) & 63), k & 1, (k >> 7) & 1
    if l == 1:
        return ((k >> 6) & 1) * 64 + (k >> 7) * 32 + ((k >> 5) & 1) * 16 + (k & 15), 0 * k, (k >> 4) & 1
    return (k >> 6) * 16 + ((k >> 1) & 15), k & 1, (k >> 5) & 1


def out_parts(k, l):
    if l == 0:
        high = ((k >> 5) & 1) * 64 + ((k >> 6) & 1) * 32
        return high + (k & 15) * 2 + ((k >> 7) & 1), k >> 8, (k >> 4) & 1
    if l == 1:
        return ((k >> 6) & 1) * 64 + (k >> 7) * 32 + (k & 31), 0 * k, (k >> 5) & 1
    return k & 127, (k >> 7) & 1, k >> 8


def select_second(u, l, n):
    i2, _, _ = in_parts(iota((n, 128), 0), l)
    rows = (i2 == iota((n, 128), 1)).astype(jnp.float32)
    j2, _, _ = out_parts(iota((128, n), 1), l)
    cols = (j2 == iota((128, n), 0)).astype(jnp.float32)
    return dot(dot_nt(rows, u[:128]), cols), dot(dot_nt(rows, u[128:]), cols)


def join_second(real, imag, l, n):
    _, s_in, c_in = in_parts(iota((n, n), 0), l)
    _, s_out, c_out = out_parts(iota((n, n), 1), l)
    full = jnp.where(c_in == c_out, real, jnp.where(c_in < c_out, imag, -imag))
    return jnp.where(s_in == s_out, full, 0.0)


def expand_second(u, l, n):
    return join_second(*select_second(u, l, n), l, n)


def permute_first(u):
    k = iota((128, 128), 1)
    pick = (iota((128, 128), 0) == (k & 15) * 8 + (k >> 4)).astype(jnp.float32)
    return dot(u, pick)


def times_i(tiles, l, roll):
    if l == 0:
        return [-tiles[1], tiles[0], -tiles[3], tiles[2]]
    step = 16 if l == 1 else 32
    real = (iota((128, 128), 1) & step) == 0
    return [jnp.where(real, -roll(t, 128 - step), roll(t, step)) for t in tiles]


def first_gate(tiles, u1, l, roll):
    both = [dot(u1, t) for t in tiles]
    turned = times_i([t[128:] for t in both], l, roll)
    return jnp.concatenate([a[:128] + b for a, b in zip(both, turned)], axis=1)


def swap_half(a, b, step, roll):
    low = (iota(a.shape, 1) & step) == 0
    return jnp.where(low, a, roll(b, step)), jnp.where(low, roll(a, 128 - step), b)


def lane_roll(x, by):
    return pltpu.roll(x, by, 1)


def kernel(state_hbm, gates_hbm, out, state, gates, s1, r1, s2, r2, s3, r3, s4, r4, m0, m1, m2, firsts, *sems):
    load, send1, recv1, send2, recv2, send3, recv3, send4, recv4, relay = sems
    wide = lax.axis_index("wide")
    narrow = lax.axis_index("narrow")
    z = narrow // 2
    rest = (narrow % 2) * 8 + wide % 8
    plane = (wide // 8) * 16 + rest

    def plane_id(p):
        return ((p // 16) * 8 + p % 8, z * 2 + (p // 8) % 2)

    def rest_id(p):
        return ((wide // 8) * 8 + p % 8, z * 2 + p // 8)

    def z_id(other):
        return (wide, other * 2 + narrow % 2)

    def z_slot(other):
        return (other % 4) * 8 + other // 4

    def signal_z(sem, step):
        for other in ((z + step) % NZ, (z + NZ - step) % NZ):
            pl.semaphore_signal(sem, inc=1, device_id=z_id(other), device_id_type=MESH)

    def relay_on(step):
        pl.semaphore_wait(relay.at[step], 2)
        if step < 3:
            signal_z(relay.at[step + 1], 2 << step)

    barrier = pltpu.get_barrier_semaphore()

    def greet(k, _):
        pl.semaphore_signal(barrier, inc=1, device_id=plane_id((plane + k) % NP), device_id_type=MESH)
        return 0

    signal_z(barrier, 1)
    lax.fori_loop(1, NP, greet, 0)
    loads = [
        pltpu.make_async_copy(gates_hbm.at[pl.ds(0, 2)], gates.at[pl.ds(0, 2)], load.at[0]),
        pltpu.make_async_copy(state_hbm, state, load.at[1]),
        pltpu.make_async_copy(gates_hbm.at[pl.ds(2, 4)], gates.at[pl.ds(2, 4)], load.at[2]),
    ]
    for copy in loads:
        copy.start()

    def exchange(source, target, own, peers, who, send, recv, h):
        def copy(p):
            return pltpu.make_async_remote_copy(
                src_ref=source(p),
                dst_ref=target,
                send_sem=send.at[h],
                recv_sem=recv.at[h],
                device_id=who(p),
                device_id_type=MESH,
            )

        pltpu.make_async_copy(source(own), target, recv.at[h]).start()

        def go(k, _):
            copy((own + k) % peers).start()
            return 0

        lax.fori_loop(1, peers, go, 0)

    def exchange_z(source, target, send, recv, h):
        def copy(p):
            return pltpu.make_async_remote_copy(
                src_ref=source.at[h, pl.ds(pl.multiple_of(p * 8, 8), 8)],
                dst_ref=target,
                send_sem=send.at[h],
                recv_sem=recv.at[h],
                device_id=z_id(p),
                device_id_type=MESH,
            )

        copy((z + 16) % NZ).start()

        def go(k, _):
            copy((z + 16 - k) % NZ).start()
            copy((z + 16 + k) % NZ).start()
            return 0

        lax.fori_loop(1, 16, go, 0)
        pltpu.make_async_copy(source.at[h, pl.ds(pl.multiple_of(z * 8, 8), 8)], target, recv.at[h]).start()

    def arrived(ref, sem):
        pltpu.make_async_copy(ref, ref, sem).wait()

    loads[0].wait()
    real, imag = select_second(gates[1], 0, 512)
    pl.semaphore_wait(barrier, 33)
    signal_z(relay.at[0], 1)
    m0[...] = join_second(real, imag, 0, 512)
    relay_on(0)
    loads[1].wait()
    loads[2].wait()
    both = first_gate([state[pl.ds(q, 128, 4), :] for q in range(4)], gates[0], 0, lane_roll)
    relay_on(1)
    for h in range(2):
        o = dot(both, m0[:, h * 256 : h * 256 + 256])
        for x in range(2):
            for p in range(8):
                a = o[p * 16 : p * 16 + 8, x * 128 : x * 128 + 128]
                b = o[p * 16 + 8 : p * 16 + 16, x * 128 : x * 128 + 128]
                s1[h, x * 16 + p], s1[h, x * 16 + 8 + p] = swap_half(a, b, 64, lane_roll)
        exchange(lambda p: s1.at[h, p], r1.at[h, plane], plane, NP, plane_id, send1, recv1, h)
    relay_on(2)
    relay_on(3)
    for h in range(2):
        arrived(r1.at[h], recv1.at[h])
        for p in range(8):
            v = [swap_half(r1[h, y * 8 + p], r1[h, 16 + y * 8 + p], 64, lane_roll) for y in range(2)]
            for c in range(2):
                pair = swap_half(v[0][c], v[1][c], 32, lane_roll)
                for b in range(2):
                    s2[h, pl.ds(c * 128 + b * 8 + p, 8, 16), :] = pair[b]
        exchange_z(s2, r2.at[h, z], send2, recv2, h)
    m1[...] = expand_second(gates[3], 1, 256)
    for t in range(2):
        firsts[t] = permute_first(gates[2 * t + 2])
    m2[...] = expand_second(gates[5], 2, 512)

    for h in range(2):
        arrived(r2.at[h], recv2.at[h])
        tiles = []
        for b in range(2):
            rows = []
            for k in range(8):
                rows += swap_half(r2[h, k * 4 + b], r2[h, k * 4 + 2 + b], 64, lane_roll)
            tiles.append(jnp.concatenate(rows, axis=0))
        o = dot(first_gate(tiles, firsts[0], 1, lane_roll), m1[...])
        for t in range(2):
            s3[h, t * 8 : t * 8 + 8] = o[:, t * 128 : t * 128 + 128].reshape(8, 16, 128)
        exchange(lambda p: s3.at[h, p], r3.at[h, rest], rest, 16, rest_id, send3, recv3, h)
        arrived(r3.at[h], recv3.at[h])
        for p in range(8):
            pair = swap_half(r3[h, p], r3[h, 8 + p], 64, lane_roll)
            for b in range(2):
                s4[h, pl.ds(b * 8 + p, 16, 16), :] = pair[b]
        exchange_z(s4, r4.at[h, z_slot(z)], send4, recv4, h)

    for h in range(2):
        arrived(r4.at[h], recv4.at[h])
    tiles = []
    for q in range(4):
        rows = []
        for k in range(8):
            rows += [r4[0, q * 8 + k], r4[1, q * 8 + k]]
        tiles.append(jnp.concatenate(rows, axis=0))
    o = dot(first_gate(tiles, firsts[1], 2, lane_roll), m2[...])
    for c in range(2):
        for s in range(2):
            q = c * 2 + s
            out[pl.ds(s * 256 + c, 128, 2), :] = o[:, q * 128 : q * 128 + 128]
    for h in range(2):
        for sent, sem in ((s1.at[h, pl.ds(0, 31)], send1), (r2.at[h, pl.ds(0, 31)], send2),
                          (s3.at[h, pl.ds(0, 15)], send3), (r4.at[h, pl.ds(0, 31)], send4)):
            pltpu.make_async_copy(sent, sent, sem.at[h]).wait()


def on_device(state, gates):
    rows = state.reshape(2, 256, 128).transpose(1, 0, 2).reshape(512, 128)
    hbm = pl.BlockSpec(memory_space=pl.ANY)
    out = pl.pallas_call(
        kernel,
        out_shape=pltpu.VMEM((512, 128), jnp.float32),
        in_specs=[hbm, hbm],
        out_specs=pl.BlockSpec(memory_space=pltpu.VMEM),
        scratch_shapes=[
            pltpu.VMEM((512, 128), jnp.float32),
            pltpu.VMEM((6, 256, 128), jnp.float32),
            pltpu.VMEM((2, NP, 8, 128), jnp.float32),
            pltpu.VMEM((2, NP, 8, 128), jnp.float32),
            pltpu.VMEM((2, NZ * 8, 128), jnp.float32),
            pltpu.VMEM((2, NZ, 8, 128), jnp.float32),
            pltpu.VMEM((2, 16, 16, 128), jnp.float32),
            pltpu.VMEM((2, 16, 16, 128), jnp.float32),
            pltpu.VMEM((2, NZ * 8, 128), jnp.float32),
            pltpu.VMEM((2, NZ, 8, 128), jnp.float32),
            pltpu.VMEM((512, 512), jnp.float32),
            pltpu.VMEM((256, 256), jnp.float32),
            pltpu.VMEM((512, 512), jnp.float32),
            pltpu.VMEM((2, 256, 128), jnp.float32),
            pltpu.SemaphoreType.DMA((3,)),
        ]
        + [pltpu.SemaphoreType.DMA((2,))] * 8
        + [pltpu.SemaphoreType.REGULAR((4,))],
        compiler_params=pltpu.CompilerParams(collective_id=0, has_side_effects=True),
        name="window",
    )(rows, gates.reshape(6, 256, 128))
    return out.reshape(256, 2, 128).transpose(1, 0, 2).reshape(2, 32768)


def solution(mesh):
    return jax.shard_map(
        on_device,
        mesh=mesh,
        in_specs=(P(None, AXES), P()),
        out_specs=P(None, AXES),
        check_vma=False,
    )
```

time: 365 us -> 87.3 us (0.24)
  blocking collectives: 125 us -> 0 us
  waiting for transfers between devices: 108 us -> 0 us
  local copies, waits for them, and re-layouts: 87 us -> 0.71 us
  Pallas kernels: 0 us -> 85.7 us
  starting transfers between devices: 40.4 us -> 0 us
    all_to_all x1 -> x0, blocking collectives: 125 us -> none  [remap(): lax.all_to_all(shaped, AXES, split_axis=0, concat_axis=0, tiled=True)]
    all_to_all x1 -> x0, waiting for transfers between devices: 108 us -> none  [remap(): lax.all_to_all(shaped, AXES, split_axis=0, concat_axis=0, tiled=True)]
    pallas_call x0 -> x1, Pallas kernels: none -> 85.7 us  [on_device(): pl.pallas_call(kernel, out_shape=pltpu.VMEM((512, 128), jnp.float32), in_...]
    another operation x6 -> x0, local copies, waits for them, and re-layouts: 46.9 us -> none  [the longest x4 46.4 us: on_device(): y = apply_layer(x.reshape(2, dim, dim, -1), gates[2 * l], gates[2 * l + 1])]
    all_to_all x1 -> x0, starting transfers between devices: 40.4 us -> none  [remap(): lax.all_to_all(shaped, AXES, split_axis=0, concat_axis=0, tiled=True)]
    reshape x2 -> x0, local copies, waits for them, and re-layouts: 34.8 us -> none  [on_device(): y = apply_layer(x.reshape(2, dim, dim, -1), gates[2 * l], gates[2 * l + 1])]
  transfers between devices with their start and end apart: 1 -> 0, of which waited for: 1 -> 0; matrix products, arithmetic and copies ran while one was open for 0% -> 0% of each run, Pallas kernels for 0% -> 0%
where the time goes in v4:
time: 87.3 us; the launch traced here: 86.4 us
  Pallas kernels  85.7 us (98%)
    pallas_call x1, Pallas kernels, on_device(): pl.pallas_call(kernel, out_shape=pltpu.VMEM((512, 128), jnp.float32), in_...  85.7 us

profile of v4, /device:TPU:24, one launch (start us, length us, event | category | flops | bytes accessed | tf_op | source)
XLA Modules:
  0.0 86.4 jit_solution(13339174719854493630)
XLA Ops:
  0.0 85.7 %window.1 = f32[512,128]{1,0:T(8,128)S(1)} custom-call(f32[512,128]{1,0:T(8,128)} %bitcast.13, f32[6,256,128]{2,1,0:T(8,128)} %bitcast.12), custom_call_target="tpu_custom_call" | custom-call | tf_op jit(solution)/shard_map/window/pallas_call | solution.py:258
  85.7 0.7 copy.6

commit v5 on v4

--- a/solution.py
+++ b/solution.py
@@ -28,39 +28,57 @@
 
 
 def in_parts(k, l):
-    if l == 0:
-        return (k >> 8) * 64 + ((k >> 1) & 63), k & 1, (k >> 7) & 1
     if l == 1:
-        return ((k >> 6) & 1) * 64 + (k >> 7) * 32 + ((k >> 5) & 1) * 16 + (k & 15), 0 * k, (k >> 4) & 1
-    return (k >> 6) * 16 + ((k >> 1) & 15), k & 1, (k >> 5) & 1
+        return ((k >> 6) & 1) * 64 + (k >> 7) * 32 + ((k >> 5) & 1) * 16 + (k & 15), (k >> 4) & 1
+    return ((k >> 4) & 1) * 64 + (k >> 7) * 32 + ((k >> 6) & 1) * 16 + (k & 15), (k >> 5) & 1
 
 
 def out_parts(k, l):
     if l == 0:
-        high = ((k >> 5) & 1) * 64 + ((k >> 6) & 1) * 32
-        return high + (k & 15) * 2 + ((k >> 7) & 1), k >> 8, (k >> 4) & 1
+        return ((k >> 5) & 1) * 64 + ((k >> 6) & 1) * 32 + (k & 15) * 2 + (k >> 7), (k >> 4) & 1
     if l == 1:
-        return ((k >> 6) & 1) * 64 + (k >> 7) * 32 + (k & 31), 0 * k, (k >> 5) & 1
-    return k & 127, (k >> 7) & 1, k >> 8
-
-
-def select_second(u, l, n):
-    i2, _, _ = in_parts(iota((n, 128), 0), l)
-    rows = (i2 == iota((n, 128), 1)).astype(jnp.float32)
-    j2, _, _ = out_parts(iota((128, n), 1), l)
-    cols = (j2 == iota((128, n), 0)).astype(jnp.float32)
-    return dot(dot_nt(rows, u[:128]), cols), dot(dot_nt(rows, u[128:]), cols)
-
-
-def join_second(real, imag, l, n):
-    _, s_in, c_in = in_parts(iota((n, n), 0), l)
-    _, s_out, c_out = out_parts(iota((n, n), 1), l)
-    full = jnp.where(c_in == c_out, real, jnp.where(c_in < c_out, imag, -imag))
-    return jnp.where(s_in == s_out, full, 0.0)
-
-
-def expand_second(u, l, n):
-    return join_second(*select_second(u, l, n), l, n)
+        return ((k >> 6) & 1) * 64 + (k >> 7) * 32 + (k & 15) * 2 + ((k >> 4) & 1), (k >> 5) & 1
+    return k & 127, k >> 7
+
+
+def expand_second(u, l):
+    i2, _ = in_parts(iota((256, 128), 0), l)
+    rows = (i2 == iota((256, 128), 1)).astype(jnp.float32)
+    j2, _ = out_parts(iota((128, 256), 1), l)
+    cols = (j2 == iota((128, 256), 0)).astype(jnp.float32)
+    real, imag = (dot(dot_nt(rows, part), cols) for part in (u[:128], u[128:]))
+    _, c_in = in_parts(iota((256, 256), 0), l)
+    _, c_out = out_parts(iota((256, 256), 1), l)
+    return jnp.where(c_in == c_out, real, jnp.where(c_in < c_out, imag, -imag))
+
+
+def second_rows(u):
+    j2, _ = out_parts(iota((256, 128), 0), 0)
+    pick = (j2 == iota((256, 128), 1)).astype(jnp.float32)
+    real, imag = dot(pick, u[:128]), dot(pick, u[128:])
+    _, c_out = out_parts(iota((256, 128), 0), 0)
+    return jnp.concatenate([jnp.where(c_out == 0, real, imag), jnp.where(c_out == 0, -imag, real)], axis=1)
+
+
+def part_s(x):
+    k = iota((256, 256), 0)
+    pick = ((k & 1) * 128 + (k >> 1) == iota((256, 256), 1)).astype(jnp.float32).astype(jnp.bfloat16)
+    high = x.astype(jnp.bfloat16)
+    left = x - high.astype(jnp.float32)
+    mid = left.astype(jnp.bfloat16)
+    low = (left - mid.astype(jnp.float32)).astype(jnp.bfloat16)
+    a, b, c = (jnp.dot(part, pick, preferred_element_type=jnp.float32) for part in (high, mid, low))
+    return (a + b) + c
+
+
+def layer_zero(tiles, u1, m):
+    re, im = (part_s(jnp.concatenate([tiles[c], tiles[2 + c]], axis=1)) for c in range(2))
+    re, im = dot(u1, re), dot(u1, im)
+    z_re, z_im = re[:128] - im[128:], im[:128] + re[128:]
+    return [
+        dot_nt(jnp.concatenate([z_re[:, k * 128 : k * 128 + 128], z_im[:, k * 128 : k * 128 + 128]], axis=1), m)
+        for k in range(2)
+    ]
 
 
 def permute_first(u):
@@ -70,8 +88,6 @@
 
 
 def times_i(tiles, l, roll):
-    if l == 0:
-        return [-tiles[1], tiles[0], -tiles[3], tiles[2]]
     step = 16 if l == 1 else 32
     real = (iota((128, 128), 1) & step) == 0
     return [jnp.where(real, -roll(t, 128 - step), roll(t, step)) for t in tiles]
@@ -80,7 +96,7 @@
 def first_gate(tiles, u1, l, roll):
     both = [dot(u1, t) for t in tiles]
     turned = times_i([t[128:] for t in both], l, roll)
-    return jnp.concatenate([a[:128] + b for a, b in zip(both, turned)], axis=1)
+    return [a[:128] + b for a, b in zip(both, turned)]
 
 
 def swap_half(a, b, step, roll):
@@ -92,7 +108,7 @@
     return pltpu.roll(x, by, 1)
 
 
-def kernel(state_hbm, gates_hbm, out, state, gates, s1, r1, s2, r2, s3, r3, s4, r4, m0, m1, m2, firsts, *sems):
+def kernel(state_hbm, gates_hbm, out, state, gates, s1, r1, s2, r2, s3, r3, s4, r4, m1, m2, firsts, *sems):
     load, send1, recv1, send2, recv2, send3, recv3, send4, recv4, relay = sems
     wide = lax.axis_index("wide")
     narrow = lax.axis_index("narrow")
@@ -127,8 +143,6 @@
         pl.semaphore_signal(barrier, inc=1, device_id=plane_id((plane + k) % NP), device_id_type=MESH)
         return 0
 
-    signal_z(barrier, 1)
-    lax.fori_loop(1, NP, greet, 0)
     loads = [
         pltpu.make_async_copy(gates_hbm.at[pl.ds(0, 2)], gates.at[pl.ds(0, 2)], load.at[0]),
         pltpu.make_async_copy(state_hbm, state, load.at[1]),
@@ -137,6 +151,8 @@
     for copy in loads:
         copy.start()
 
+    signal_z(barrier, 1)
+    lax.fori_loop(1, NP, greet, 0)
     def exchange(source, target, own, peers, who, send, recv, h):
         def copy(p):
             return pltpu.make_async_remote_copy(
@@ -156,8 +172,9 @@
 
         lax.fori_loop(1, peers, go, 0)
 
-    def exchange_z(source, target, send, recv, h):
+    def exchange_z(source, target, send, recv, h, first=0, last=16):
         def copy(p):
+            p = p % NZ
             return pltpu.make_async_remote_copy(
                 src_ref=source.at[h, pl.ds(pl.multiple_of(p * 8, 8), 8)],
                 dst_ref=target,
@@ -167,39 +184,38 @@
                 device_id_type=MESH,
             )
 
-        copy((z + 16) % NZ).start()
-
         def go(k, _):
-            copy((z + 16 - k) % NZ).start()
-            copy((z + 16 + k) % NZ).start()
+            copy(z + 16 - k).start()
+            copy(z + 16 + k).start()
             return 0
 
-        lax.fori_loop(1, 16, go, 0)
+        if first == 0:
+            copy(z + 16).start()
+        lax.fori_loop(max(first, 1), last, go, 0)
+        if first > 0:
+            return
         pltpu.make_async_copy(source.at[h, pl.ds(pl.multiple_of(z * 8, 8), 8)], target, recv.at[h]).start()
 
     def arrived(ref, sem):
         pltpu.make_async_copy(ref, ref, sem).wait()
 
     loads[0].wait()
-    real, imag = select_second(gates[1], 0, 512)
-    pl.semaphore_wait(barrier, 33)
-    signal_z(relay.at[0], 1)
-    m0[...] = join_second(real, imag, 0, 512)
-    relay_on(0)
+    m0 = second_rows(gates[1])
     loads[1].wait()
-    loads[2].wait()
-    both = first_gate([state[pl.ds(q, 128, 4), :] for q in range(4)], gates[0], 0, lane_roll)
-    relay_on(1)
-    for h in range(2):
-        o = dot(both, m0[:, h * 256 : h * 256 + 256])
+    halves = layer_zero([state[pl.ds(q, 128, 4), :] for q in range(4)], gates[0], m0)
+    for h in range(2):
+        o = halves[h]
         for x in range(2):
             for p in range(8):
                 a = o[p * 16 : p * 16 + 8, x * 128 : x * 128 + 128]
                 b = o[p * 16 + 8 : p * 16 + 16, x * 128 : x * 128 + 128]
                 s1[h, x * 16 + p], s1[h, x * 16 + 8 + p] = swap_half(a, b, 64, lane_roll)
+    pl.semaphore_wait(barrier, 33)
+    signal_z(relay.at[0], 1)
+    for h in range(2):
         exchange(lambda p: s1.at[h, p], r1.at[h, plane], plane, NP, plane_id, send1, recv1, h)
+        relay_on(h)
     relay_on(2)
-    relay_on(3)
     for h in range(2):
         arrived(r1.at[h], recv1.at[h])
         for p in range(8):
@@ -208,11 +224,17 @@
                 pair = swap_half(v[0][c], v[1][c], 32, lane_roll)
                 for b in range(2):
                     s2[h, pl.ds(c * 128 + b * 8 + p, 8, 16), :] = pair[b]
-        exchange_z(s2, r2.at[h, z], send2, recv2, h)
-    m1[...] = expand_second(gates[3], 1, 256)
+        if h == 0:
+            exchange_z(s2, r2.at[h, z], send2, recv2, h, 8, 16)
+            relay_on(3)
+            exchange_z(s2, r2.at[h, z], send2, recv2, h, 0, 8)
+        else:
+            exchange_z(s2, r2.at[h, z], send2, recv2, h)
+    loads[2].wait()
+    m1[...] = expand_second(gates[3], 1)
     for t in range(2):
         firsts[t] = permute_first(gates[2 * t + 2])
-    m2[...] = expand_second(gates[5], 2, 512)
+    m2[...] = expand_second(gates[5], 2)
 
     for h in range(2):
         arrived(r2.at[h], recv2.at[h])
@@ -222,7 +244,7 @@
             for k in range(8):
                 rows += swap_half(r2[h, k * 4 + b], r2[h, k * 4 + 2 + b], 64, lane_roll)
             tiles.append(jnp.concatenate(rows, axis=0))
-        o = dot(first_gate(tiles, firsts[0], 1, lane_roll), m1[...])
+        o = dot(jnp.concatenate(first_gate(tiles, firsts[0], 1, lane_roll), axis=1), m1[...])
         for t in range(2):
             s3[h, t * 8 : t * 8 + 8] = o[:, t * 128 : t * 128 + 128].reshape(8, 16, 128)
         exchange(lambda p: s3.at[h, p], r3.at[h, rest], rest, 16, rest_id, send3, recv3, h)
@@ -241,11 +263,13 @@
         for k in range(8):
             rows += [r4[0, q * 8 + k], r4[1, q * 8 + k]]
         tiles.append(jnp.concatenate(rows, axis=0))
-    o = dot(first_gate(tiles, firsts[1], 2, lane_roll), m2[...])
+    lows = [swap_half(tiles[k], tiles[k + 2], 16, lane_roll) for k in range(2)]
+    y = first_gate([lows[0][0], lows[1][0], lows[0][1], lows[1][1]], firsts[1], 2, lane_roll)
+    wide_y = jnp.concatenate([jnp.concatenate(y[:2], axis=1), jnp.concatenate(y[2:], axis=1)], axis=0)
+    o = dot(wide_y, m2[...])
     for c in range(2):
-        for s in range(2):
-            q = c * 2 + s
-            out[pl.ds(s * 256 + c, 128, 2), :] = o[:, q * 128 : q * 128 + 128]
+        for k in range(2):
+            out[pl.ds(k * 256 + c, 128, 2), :] = o[k * 128 : k * 128 + 128, c * 128 : c * 128 + 128]
     for h in range(2):
         for sent, sem in ((s1.at[h, pl.ds(0, 31)], send1), (r2.at[h, pl.ds(0, 31)], send2),
                           (s3.at[h, pl.ds(0, 15)], send3), (r4.at[h, pl.ds(0, 31)], send4)):
@@ -271,9 +295,8 @@
             pltpu.VMEM((2, 16, 16, 128), jnp.float32),
             pltpu.VMEM((2, NZ * 8, 128), jnp.float32),
             pltpu.VMEM((2, NZ, 8, 128), jnp.float32),
-            pltpu.VMEM((512, 512), jnp.float32),
             pltpu.VMEM((256, 256), jnp.float32),
-            pltpu.VMEM((512, 512), jnp.float32),
+            pltpu.VMEM((256, 256), jnp.float32),
             pltpu.VMEM((2, 256, 128), jnp.float32),
             pltpu.SemaphoreType.DMA((3,)),
         ]

time: 87.3 us -> 87 us (level)
  no operation moved by 1% of the time
where the time goes in v5:
time: 87 us; the launch traced here: 85.6 us
  Pallas kernels  84.9 us (98%)
    pallas_call x1, Pallas kernels, on_device(): pl.pallas_call(kernel, out_shape=pltpu.VMEM((512, 128), jnp.float32), in_...  84.9 us

profile of v5, /device:TPU:24, one launch (start us, length us, event | category | flops | bytes accessed | tf_op | source)
XLA Modules:
  0.0 85.6 jit_solution(11355127135453730600)
XLA Ops:
  0.0 84.9 %window.1 = f32[512,128]{1,0:T(8,128)S(1)} custom-call(f32[512,128]{1,0:T(8,128)} %bitcast.13, f32[6,256,128]{2,1,0:T(8,128)} %bitcast.12), custom_call_target="tpu_custom_call" | custom-call | tf_op jit(solution)/shard_map/window/pallas_call | solution.py:282
  84.9 0.7 copy.6

commit v6 on v5

--- a/solution.py
+++ b/solution.py
@@ -216,7 +216,8 @@
         exchange(lambda p: s1.at[h, p], r1.at[h, plane], plane, NP, plane_id, send1, recv1, h)
         relay_on(h)
     relay_on(2)
-    for h in range(2):
+
+    def pack(h):
         arrived(r1.at[h], recv1.at[h])
         for p in range(8):
             v = [swap_half(r1[h, y * 8 + p], r1[h, 16 + y * 8 + p], 64, lane_roll) for y in range(2)]
@@ -224,12 +225,14 @@
                 pair = swap_half(v[0][c], v[1][c], 32, lane_roll)
                 for b in range(2):
                     s2[h, pl.ds(c * 128 + b * 8 + p, 8, 16), :] = pair[b]
-        if h == 0:
-            exchange_z(s2, r2.at[h, z], send2, recv2, h, 8, 16)
-            relay_on(3)
-            exchange_z(s2, r2.at[h, z], send2, recv2, h, 0, 8)
-        else:
-            exchange_z(s2, r2.at[h, z], send2, recv2, h)
+
+    pack(0)
+    exchange_z(s2, r2.at[0, z], send2, recv2, 0, 8, 12)
+    pack(1)
+    relay_on(3)
+    exchange_z(s2, r2.at[0, z], send2, recv2, 0, 0, 8)
+    exchange_z(s2, r2.at[0, z], send2, recv2, 0, 12, 16)
+    exchange_z(s2, r2.at[1, z], send2, recv2, 1, 0, 16)
     loads[2].wait()
     m1[...] = expand_second(gates[3], 1)
     for t in range(2):

time: 87 us -> 86.1 us (0.990)
  no operation moved by 1% of the time
where the time goes in v6:
time: 86.1 us; the launch traced here: 85.1 us
  Pallas kernels  84.4 us (98%)
    pallas_call x1, Pallas kernels, on_device(): pl.pallas_call(kernel, out_shape=pltpu.VMEM((512, 128), jnp.float32), in_...  84.4 us

profile of v6, /device:TPU:24, one launch (start us, length us, event | category | flops | bytes accessed | tf_op | source)
XLA Modules:
  0.0 85.1 jit_solution(9394529485904898743)
XLA Ops:
  0.0 84.4 %window.1 = f32[512,128]{1,0:T(8,128)S(1)} custom-call(f32[512,128]{1,0:T(8,128)} %bitcast.13, f32[6,256,128]{2,1,0:T(8,128)} %bitcast.12), custom_call_target="tpu_custom_call" | custom-call | tf_op jit(solution)/shard_map/window/pallas_call | solution.py:285
  84.4 0.7 copy.6

commit v7 on v6

--- a/solution.py
+++ b/solution.py
@@ -21,6 +21,17 @@
     return lax.dot_general(
         a, b, (((1,), (1,)), ((), ())), precision=lax.Precision.HIGHEST, preferred_element_type=jnp.float32
     )
+
+
+def two_parts(x):
+    high = x.astype(jnp.bfloat16)
+    return high, (x - high.astype(jnp.float32)).astype(jnp.bfloat16)
+
+
+def dot3(a, b, dims=((1,), (0,))):
+    (ah, al), (bh, bl) = two_parts(a), two_parts(b)
+    one = lambda p, q: lax.dot_general(p, q, (dims, ((), ())), preferred_element_type=jnp.float32)
+    return one(ah, bh) + (one(ah, bl) + one(al, bh))
 
 
 def iota(shape, dim):
@@ -73,10 +84,10 @@
 
 def layer_zero(tiles, u1, m):
     re, im = (part_s(jnp.concatenate([tiles[c], tiles[2 + c]], axis=1)) for c in range(2))
-    re, im = dot(u1, re), dot(u1, im)
+    re, im = dot3(u1, re), dot3(u1, im)
     z_re, z_im = re[:128] - im[128:], im[:128] + re[128:]
     return [
-        dot_nt(jnp.concatenate([z_re[:, k * 128 : k * 128 + 128], z_im[:, k * 128 : k * 128 + 128]], axis=1), m)
+        dot3(jnp.concatenate([z_re[:, k * 128 : k * 128 + 128], z_im[:, k * 128 : k * 128 + 128]], axis=1), m, ((1,), (1,)))
         for k in range(2)
     ]
 
@@ -94,7 +105,7 @@
 
 
 def first_gate(tiles, u1, l, roll):
-    both = [dot(u1, t) for t in tiles]
+    both = [dot3(u1, t) for t in tiles]
     turned = times_i([t[128:] for t in both], l, roll)
     return [a[:128] + b for a, b in zip(both, turned)]
 
@@ -247,7 +258,7 @@
             for k in range(8):
                 rows += swap_half(r2[h, k * 4 + b], r2[h, k * 4 + 2 + b], 64, lane_roll)
             tiles.append(jnp.concatenate(rows, axis=0))
-        o = dot(jnp.concatenate(first_gate(tiles, firsts[0], 1, lane_roll), axis=1), m1[...])
+        o = dot3(jnp.concatenate(first_gate(tiles, firsts[0], 1, lane_roll), axis=1), m1[...])
         for t in range(2):
             s3[h, t * 8 : t * 8 + 8] = o[:, t * 128 : t * 128 + 128].reshape(8, 16, 128)
         exchange(lambda p: s3.at[h, p], r3.at[h, rest], rest, 16, rest_id, send3, recv3, h)
@@ -269,7 +280,7 @@
     lows = [swap_half(tiles[k], tiles[k + 2], 16, lane_roll) for k in range(2)]
     y = first_gate([lows[0][0], lows[1][0], lows[0][1], lows[1][1]], firsts[1], 2, lane_roll)
     wide_y = jnp.concatenate([jnp.concatenate(y[:2], axis=1), jnp.concatenate(y[2:], axis=1)], axis=0)
-    o = dot(wide_y, m2[...])
+    o = dot3(wide_y, m2[...])
     for c in range(2):
         for k in range(2):
             out[pl.ds(k * 256 + c, 128, 2), :] = o[k * 128 : k * 128 + 128, c * 128 : c * 128 + 128]

time: 86.1 us -> 85.7 us (level)
  Pallas kernels: 84.4 us -> 83.5 us
    pallas_call x1, Pallas kernels: 84.4 us -> 83.5 us  [on_device(): pl.pallas_call(kernel, out_shape=pltpu.VMEM((512, 128), jnp.float32), in_...]
where the time goes in v7:
time: 85.7 us; the launch traced here: 84.2 us
  Pallas kernels  83.5 us (97%)
    pallas_call x1, Pallas kernels, on_device(): pl.pallas_call(kernel, out_shape=pltpu.VMEM((512, 128), jnp.float32), in_...  83.5 us

profile of v7, /device:TPU:24, one launch (start us, length us, event | category | flops | bytes accessed | tf_op | source)
XLA Modules:
  0.0 84.2 jit_solution(7241545373091107981)
XLA Ops:
  0.0 83.5 %window.1 = f32[512,128]{1,0:T(8,128)S(1)} custom-call(f32[512,128]{1,0:T(8,128)} %bitcast.13, f32[6,256,128]{2,1,0:T(8,128)} %bitcast.12), custom_call_target="tpu_custom_call" | custom-call | tf_op jit(solution)/shard_map/window/pallas_call | solution.py:296
  83.5 0.7 copy.6
